TPU v7x, 32 devices: a whole 2x2x4 slice. The times are simulated.
32 devices in a mesh: bins: 2 (over x), fsdp: 16 (over z, y, core).
Axes of the slice: x: 2, y: 2, z: 4, core: 2. Of those that a mesh axis runs over, the one named last changes fastest.
Arguments:
- tokens: bfloat16 [16384, 1152], P(('bins', 'fsdp')), may hold values from -6 to 6
- condition: float32 [2, 1152], P('bins'), may hold values from -6 to 6
- segments: int32 [16384], P('bins'), may hold values from 0 to 63, as said below
- cotangent: bfloat16 [16384, 1152], P(('bins', 'fsdp')), may hold values from -6 to 6
- target: bfloat16 [16384, 768], P(('bins', 'fsdp')), may hold values from -6 to 6
- w_ada: bfloat16 [1152, 6912], P(None, 'fsdp'), may hold values from -0.1875 to 0.1875
- w_qkv: bfloat16 [1152, 3456], P('fsdp'), may hold values from -0.1875 to 0.1875
- w_out: bfloat16 [1152, 1152], P('fsdp'), may hold values from -0.75 to 0.75
- w_fc1: bfloat16 [1152, 4608], P('fsdp'), may hold values from -0.1875 to 0.1875
- w_fc2: bfloat16 [4608, 1152], P('fsdp'), may hold values from -0.09375 to 0.09375
- w_proj1: bfloat16 [1152, 2048], P('fsdp'), may hold values from -0.1875 to 0.1875
- w_proj2: bfloat16 [2048, 2048], P('fsdp'), may hold values from -0.125 to 0.125
- w_proj3: bfloat16 [2048, 768], P('fsdp'), may hold values from -0.125 to 0.125
Outputs:
- output: bfloat16 [16384, 1152], P(('bins', 'fsdp'))
- grad_tokens: float32 [16384, 1152], P(('bins', 'fsdp'))
- grad_condition: float32 [2, 1152], P('bins')
- grad_ada: float32 [1152, 6912], P(None, 'fsdp')
- grad_qkv: float32 [1152, 3456], P('fsdp')
- grad_out: float32 [1152, 1152], P('fsdp')
- grad_fc1: float32 [1152, 4608], P('fsdp')
- grad_fc2: float32 [4608, 1152], P('fsdp')
- grad_proj1: float32 [1152, 2048], P('fsdp')
- grad_proj2: float32 [2048, 2048], P('fsdp')
- grad_proj3: float32 [2048, 768], P('fsdp')
Inputs may be any that keep to these rules, and one draw needn't show every extreme that they name: segments never fall; each aligned block of 1024 tokens holds either one image of 1024 tokens or four images of 256 tokens; images of different blocks have different ids; the first block holds one image and the last block four.
All inputs are finite; a program needn't handle non-finite values.
Results may differ from a plain program's by a relative error of at most 0.015.
Values may be sent and summed in bfloat16 or wider, within the bound.
No kernel may reach another device: no remote copies, remote signals or barrier semaphores. Data moves between devices by JAX's collectives and lax.ppermute only.
A program may use at most 320 MiB of HBM per device.

v0:
```python
from functools import partial
import jax
import jax.numpy as jnp
from jax import lax
from jax.sharding import PartitionSpec as P

HEADS = 16
HIGH = lax.Precision.HIGHEST


def swapped(block, axis, apart):
    count = lax.axis_size(axis)
    route = []
    for low in range(count):
        high = low | 1 << apart
        if high != low and high < count:
            route += [(low, high), (high, low)]
    return lax.ppermute(block, axis, route)


def bins_peer(block):
    return lax.ppermute(block, "bins", [(0, 1), (1, 0)])


def hop(block, apart):
    chips = lax.axis_size("fsdp") // 2
    route = [2 * chip for chip in range(chips // 2)]
    route = route + [chip + 1 for chip in reversed(route)]
    pairs = []
    for spot, chip in enumerate(route):
        onward = route[(spot + apart) % chips]
        pairs += [(2 * chip, 2 * onward), (2 * chip + 1, 2 * onward + 1)]
    return lax.ppermute(block, "fsdp", pairs)


def chip_at(apart):
    chips = lax.axis_size("fsdp") // 2
    chip = lax.axis_index("fsdp") // 2
    spot = jnp.where(chip % 2 == 0, chip // 2, chips - 1 - chip // 2)
    spot = (spot + apart) % chips
    return jnp.where(spot < chips // 2, 2 * spot, 2 * (chips - 1 - spot) + 1)


def doubled(block):
    count, place = (lax.axis_size("fsdp"), lax.axis_index("fsdp"))
    step = 0
    while 1 << step < count:
        other = swapped(block, "fsdp", step)
        upper = (place >> step) % 2 == 1
        block = jnp.where(upper, jnp.concatenate([other, block]), jnp.concatenate([block, other]))
        step += 1
    return block


def halved(block):
    count, place = (lax.axis_size("fsdp"), lax.axis_index("fsdp"))
    step = count.bit_length() - 1
    while step:
        step -= 1
        upper = (place >> step) % 2
        length = block.shape[0] // 2
        sent = lax.dynamic_slice_in_dim(block, (1 - upper) * length, length)
        kept = lax.dynamic_slice_in_dim(block, upper * length, length)
        block = kept + swapped(sent, "fsdp", step)
    return block


def group_sum(block):
    step = 0
    while 1 << step < lax.axis_size("fsdp"):
        block = block + swapped(block, "fsdp", step)
        step += 1
    return block


def core_rows(turned, core):
    chips = lax.axis_size("fsdp") // 2
    split = turned.reshape(chips, 2, -1, turned.shape[-1])
    picked = lax.dynamic_index_in_dim(split, core, 1, keepdims=False)
    return picked.reshape(-1, turned.shape[-1])


def chip_grad(left, right):
    core = lax.axis_index("fsdp") % 2
    turned = left.T
    mine = core_rows(turned, core)
    theirs = swapped(core_rows(turned, 1 - core), "fsdp", 0)
    rows = jnp.concatenate([mine, theirs], axis=1)
    grads = jnp.concatenate([right, swapped(right, "fsdp", 0)], axis=0)
    total = jnp.dot(rows, grads, preferred_element_type=jnp.float32)
    return total.reshape(lax.axis_size("fsdp") // 2, -1, right.shape[1])


def ring_sum(parts):
    chips, rows = parts.shape[:2]
    far = chips // 2
    cut = (rows // 2 + 7) // 8 * 8

    def part(apart):
        return lax.dynamic_index_in_dim(parts, chip_at(apart), 0, keepdims=False)

    def low(block):
        return block.astype(jnp.bfloat16)

    last = part(far)
    onward = hop(low(last[:cut]), 1)
    back = hop(low(last[cut:]), -1)
    for apart in range(far - 1, 0, -1):
        ahead, behind = (part(apart), part(-apart))
        if apart == far - 1:
            ahead = jnp.concatenate([ahead[:cut] + onward, ahead[cut:]])
            behind = jnp.concatenate([behind[:cut], behind[cut:] + back])
        else:
            ahead, behind = (ahead + onward, behind + back)
        onward, back = (hop(low(ahead), 1), hop(low(behind), -1))
    return part(0) + onward + back


def both_groups(block):
    rounded = lax.reduce_precision(block, 8, 7)
    return rounded + bins_peer(rounded.astype(jnp.bfloat16)).astype(jnp.float32)


def full_grad(left, right):
    return both_groups(ring_sum(chip_grad(left, right)))


def modulate(values, shift, scale):
    center = values - jnp.mean(values, axis=-1, keepdims=True)
    spread = jnp.mean(center * center, axis=-1, keepdims=True)
    return center * lax.rsqrt(spread + 1e-06) * (1.0 + scale) + shift


def cosine_sum(target_f, predicted):
    dots = jnp.sum(predicted * target_f, axis=-1)
    first = lax.rsqrt(jnp.sum(predicted * predicted, axis=-1) + 1e-06)
    second = lax.rsqrt(jnp.sum(target_f * target_f, axis=-1) + 1e-06)
    return jnp.sum(dots * first * second)


def product(left, right):
    return jnp.dot(left, right, preferred_element_type=jnp.float32)


def input_grad(grad, weight):
    return jnp.einsum("ne,de->nd", grad, weight, preferred_element_type=jnp.float32)


def shards(
    tokens,
    condition,
    segments,
    cotangent,
    target,
    w_ada,
    w_qkv,
    w_out,
    w_fc1,
    w_fc2,
    w_proj1,
    w_proj2,
    w_proj3,
):
    count = tokens.shape[0]
    width = tokens.shape[1]
    head_size = width // HEADS
    factor = head_size ** (-0.5)
    tokens_f = tokens.astype(jnp.float32)
    target_f = target.astype(jnp.float32)
    silu_cond, silu_back = jax.vjp(jax.nn.silu, condition)
    cond_low = silu_cond.astype(jnp.bfloat16)
    mod_cols = product(cond_low, w_ada)
    modulation = doubled(mod_cols.reshape(-1)).reshape(6, width)
    block_set = (
        lax.all_gather(w_qkv, "fsdp", axis=0, tiled=True),
        lax.all_gather(w_out, "fsdp", axis=0, tiled=True),
        lax.all_gather(w_fc1, "fsdp", axis=0, tiled=True),
        lax.all_gather(w_fc2, "fsdp", axis=0, tiled=True),
    )
    head_set = (
        lax.all_gather(w_proj1, "fsdp", axis=0, tiled=True),
        lax.all_gather(w_proj2, "fsdp", axis=0, tiled=True),
        lax.all_gather(w_proj3, "fsdp", axis=0, tiled=True),
    )
    full_qkv, full_out, full_fc1, full_fc2 = block_set
    head_first, head_second, head_third = head_set
    h_one, norm_one_back = jax.vjp(modulate, tokens_f, modulation[0], modulation[1])
    in_one = h_one.astype(jnp.bfloat16)
    qkv_low = product(in_one, full_qkv).astype(jnp.bfloat16).reshape(count, 3, HEADS, head_size)
    queries = qkv_low[:, 0]
    pair_own = jnp.stack([qkv_low[:, 1], qkv_low[:, 2]])
    pair_peer = swapped(pair_own, "fsdp", 0)
    keys_all = jnp.concatenate([pair_own[0], pair_peer[0]], axis=0)
    values_all = jnp.concatenate([pair_own[1], pair_peer[1]], axis=0)
    place = lax.axis_index("fsdp")
    own_ids = lax.dynamic_slice_in_dim(segments, place * count, count)
    peer_ids = lax.dynamic_slice_in_dim(segments, jnp.bitwise_xor(place, 1) * count, count)
    same = own_ids[:, None] == jnp.concatenate([own_ids, peer_ids])[None, :]
    raw = jnp.einsum("qhd,khd->hqk", queries, keys_all, preferred_element_type=jnp.float32) * factor
    masked = jnp.where(same[None], raw, -1e30)
    highest = jnp.max(masked, axis=-1, keepdims=True)
    expo = jnp.exp(masked - highest)
    totals = jnp.sum(expo, axis=-1, keepdims=True)
    log_total = highest + jnp.log(totals)
    probs_low = (expo / totals).astype(jnp.bfloat16)
    attended = jnp.einsum("hqk,khd->qhd", probs_low, values_all, preferred_element_type=jnp.float32)
    attended = attended.astype(jnp.bfloat16).reshape(count, width)
    branch_one = product(attended, full_out)
    resid_one = tokens_f + modulation[2] * branch_one
    h_two, norm_two_back = jax.vjp(modulate, resid_one, modulation[3], modulation[4])
    in_two = h_two.astype(jnp.bfloat16)
    hidden_pre = product(in_two, full_fc1)
    hidden_act, gelu_back = jax.vjp(partial(jax.nn.gelu, approximate=True), hidden_pre)
    hidden_low = hidden_act.astype(jnp.bfloat16)
    branch_two = product(hidden_low, full_fc2)
    result = resid_one + modulation[5] * branch_two
    result_low = result.astype(jnp.bfloat16)
    first_act, first_back = jax.vjp(jax.nn.silu, product(result_low, head_first))
    first_low = first_act.astype(jnp.bfloat16)
    second_act, second_back = jax.vjp(jax.nn.silu, product(first_low, head_second))
    second_low = second_act.astype(jnp.bfloat16)
    predicted = product(second_low, head_third)
    cos_total, cos_back = jax.vjp(partial(cosine_sum, target_f), predicted)
    (grad_pred,) = cos_back(jnp.float32(-1.0))
    grad_pred_low = grad_pred.astype(jnp.bfloat16)
    grad_third = full_grad(second_low, grad_pred_low)
    (grad_second_pre,) = second_back(input_grad(grad_pred_low, head_third))
    grad_second_low = grad_second_pre.astype(jnp.bfloat16)
    grad_second = full_grad(first_low, grad_second_low)
    (grad_first_pre,) = first_back(input_grad(grad_second_low, head_second))
    grad_first_low = grad_first_pre.astype(jnp.bfloat16)
    grad_first = full_grad(result_low, grad_first_low)
    d_result = cotangent.astype(jnp.float32) + input_grad(grad_first_low, head_first)
    grad_gate_two = jnp.sum(d_result * branch_two, axis=0)
    d_branch_two = (d_result * modulation[5]).astype(jnp.bfloat16)
    grad_fc2 = full_grad(hidden_low, d_branch_two)
    (d_pre,) = gelu_back(input_grad(d_branch_two, full_fc2))
    d_pre_low = d_pre.astype(jnp.bfloat16)
    grad_fc1 = full_grad(in_two, d_pre_low)
    d_resid_part, grad_shift_two, grad_scale_two = norm_two_back(input_grad(d_pre_low, full_fc1))
    d_resid = d_result + d_resid_part
    grad_gate_one = jnp.sum(d_resid * branch_one, axis=0)
    d_branch_one = (d_resid * modulation[2]).astype(jnp.bfloat16)
    grad_out = full_grad(attended, d_branch_one)
    d_attended = (
        input_grad(d_branch_one, full_out).astype(jnp.bfloat16).reshape(count, HEADS, head_size)
    )
    again_raw = (
        jnp.einsum("qhd,khd->hqk", queries, keys_all, preferred_element_type=jnp.float32) * factor
    )
    probs = jnp.exp(jnp.where(same[None], again_raw, -1e30) - log_total)
    probs_again = probs.astype(jnp.bfloat16)
    d_probs = jnp.einsum("qhd,khd->hqk", d_attended, values_all, preferred_element_type=jnp.float32)
    centre = jnp.sum(d_probs * probs, axis=-1, keepdims=True)
    d_scores = (probs * (d_probs - centre)).astype(jnp.bfloat16)
    d_queries = (
        jnp.einsum("hqk,khd->qhd", d_scores, keys_all, preferred_element_type=jnp.float32) * factor
    )
    d_keys = (
        jnp.einsum("hqk,qhd->khd", d_scores, queries, preferred_element_type=jnp.float32) * factor
    )
    d_values = jnp.einsum(
        "hqk,qhd->khd", probs_again, d_attended, preferred_element_type=jnp.float32
    )
    from_peer = swapped(jnp.stack([d_keys[count:], d_values[count:]]), "fsdp", 0)
    keys_grad = d_keys[:count] + from_peer[0]
    values_grad = d_values[:count] + from_peer[1]
    d_qkv = (
        jnp.stack([d_queries, keys_grad, values_grad], axis=1)
        .reshape(count, 3 * width)
        .astype(jnp.bfloat16)
    )
    grad_qkv = full_grad(in_one, d_qkv)
    d_tok_part, grad_shift_one, grad_scale_one = norm_one_back(input_grad(d_qkv, full_qkv))
    grad_tokens = d_resid + d_tok_part
    d_modulation = jnp.stack(
        [
            grad_shift_one,
            grad_scale_one,
            grad_gate_one,
            grad_shift_two,
            grad_scale_two,
            grad_gate_two,
        ]
    ).reshape(6 * width)
    mod_grad_cols = halved(d_modulation).reshape(1, -1)
    cond_part = jnp.dot(mod_grad_cols, w_ada.astype(jnp.float32).T, precision=HIGH)
    (grad_condition,) = silu_back(group_sum(cond_part))
    group = lax.axis_index("bins")
    cond_low_f = cond_low.astype(jnp.float32)
    other_cond, other_cols = (bins_peer(cond_low_f), bins_peer(mod_grad_cols))
    first_cond = jnp.where(group == 0, cond_low_f, other_cond)
    last_cond = jnp.where(group == 0, other_cond, cond_low_f)
    first_cols = jnp.where(group == 0, mod_grad_cols, other_cols)
    last_cols = jnp.where(group == 0, other_cols, mod_grad_cols)
    grad_ada = first_cond.T * first_cols + last_cond.T * last_cols
    return (
        result_low,
        grad_tokens,
        grad_condition,
        grad_ada,
        grad_qkv,
        grad_out,
        grad_fc1,
        grad_fc2,
        grad_first,
        grad_second,
        grad_third,
    )


def solution(mesh):
    placed = (
        P(("bins", "fsdp"), None),
        P("bins", None),
        P("bins"),
        P(("bins", "fsdp"), None),
        P(("bins", "fsdp"), None),
        P(None, "fsdp"),
        P("fsdp", None),
        P("fsdp", None),
        P("fsdp", None),
        P("fsdp", None),
        P("fsdp", None),
        P("fsdp", None),
        P("fsdp", None),
    )
    return jax.shard_map(
        shards,
        mesh=mesh,
        in_specs=placed,
        out_specs=(
            P(("bins", "fsdp"), None),
            P(("bins", "fsdp"), None),
            P("bins", None),
            P(None, "fsdp"),
            P("fsdp", None),
            P("fsdp", None),
            P("fsdp", None),
            P("fsdp", None),
            P("fsdp", None),
            P("fsdp", None),
            P("fsdp", None),
        ),
        check_vma=False,
    )
```

profile of v0, /device:TPU:0, one launch (start us, length us, event | category | flops | bytes accessed | tf_op | source)
XLA Modules:
  0.0 1121.1 jit_solution(2670835607985499530)
XLA Ops:
  27.0 58.8 %all-gather.8.cloned.1.call-done = bf16[1152,3456]{1,0:T(8,128)(2,1)} async-done(((bf16[72,3456]{1,0:T(8,128)(2,1)}), bf16[1152,3456]{1,0:T(8,128)(2,1)}) %all-gather.8.cloned.1.call-update) | async-done | bytes 7962640 | tf_op jit(solution)/shard_map/all_gather | solution.py:175
  85.8 9.9 convolution_convert_fusion
  114.2 16.7 %fusion.244 = (f32[16,512]{1,0:T(8,128)S(1)}, f32[16,512,1024]{2,1,0:T(8,128)}) fusion(bf16[512,16,72]{0,2,1:T(8,128)(2,1)S(1)} %get-tuple-element.67, bf16[512,16,72]{0,2,1:T(8,128)(2,1)S(1)} %get-tuple-element.54, bf16[512,3,16,72]{0,3,2,1:T(8,128)(2,1)} %bitcast.488, pred[512,1024]{1,0:T(8,128)(4,1)S(1)} %copy-done.46), kind=kOutput, calls=%fused_computation.452 | convolution fusion | flops 1237835776 | bytes 37650432 | tf_op jit(solution)/shard_map/qhd,khd->hqk/dot_general | solution.py:199
  130.8 14.6 %fusion = f32[16,512]{1,0:T(8,128)S(1)} fusion(f32[16,512,1024]{2,1,0:T(8,128)} %get-tuple-element.101, f32[16,512]{1,0:T(8,128)S(1)} %get-tuple-element.100), kind=kLoop, calls=%fused_computation.6 | loop fusion | flops 16769024 | bytes 33619968 | tf_op jit(solution)/shard_map/reduce_sum | solution.py:203
  146.1 14.9 %fusion.98 = bf16[16,72,512]{2,1,0:T(8,128)(2,1)S(1)} fusion(f32[16,512,1024]{2,1,0:T(8,128)} %get-tuple-element.101, f32[16,512]{1,0:T(8,128)S(1)} %fusion, f32[16,512]{1,0:T(8,128)S(1)} %get-tuple-element.100, bf16[512,16,72]{0,2,1:T(8,128)(2,1)} %get-tuple-element.66, bf16[512,16,72]{0,2,1:T(8,128)(2,1)} %get-tuple-element.52), kind=kOutput, calls=%fused_computation.150 | convolution fusion | flops 1238433792 | bytes 37158912 | tf_op jit(solution)/shard_map/hqk,khd->qhd/dot_general | solution.py:206
  168.2 51.1 %all-gather.12.cloned.1.call-done = bf16[1152,4608]{1,0:T(8,128)(2,1)} async-done(((bf16[72,4608]{1,0:T(8,128)(2,1)}), bf16[1152,4608]{1,0:T(8,128)(2,1)}) %all-gather.12.cloned.1.call-update) | async-done | bytes 10616848 | tf_op jit(solution)/shard_map/all_gather | solution.py:177
  219.3 15.4 %fusion.20 = (bf16[4608,512]{0,1:T(8,128)(2,1)}, f32[512,4608]{1,0:T(8,128)}) fusion(bf16[1152,4608]{1,0:T(8,128)(2,1)} %all-gather.12.cloned.1.call-done, f32[512,1152]{1,0:T(8,128)} %copy-done.5, f32[1152]{0:T(1024)S(1)} %get-tuple-element.91, f32[1152]{0:T(1024)S(1)} %get-tuple-element.92, f32[512]{0:T(512)S(1)} %fusion.216, ...), kind=kOutput, calls=%fused_computation.28 | convolution fusion | flops 5460000768 | bytes 27145216 | tf_op jit(solution)/shard_map/dot_general | solution.py:142
  234.8 73.6 %all-gather.14.cloned.1.call-done = bf16[4608,1152]{1,0:T(8,128)(2,1)} async-done(((bf16[288,1152]{1,0:T(8,128)(2,1)}), bf16[4608,1152]{1,0:T(8,128)(2,1)}) %all-gather.14.cloned.1.call-update) | async-done | bytes 10616848 | tf_op jit(solution)/shard_map/all_gather | solution.py:178
  308.4 14.1 %add_convert_fusion = (bf16[512,1152]{1,0:T(8,128)(2,1)}, f32[512,1152]{1,0:T(8,128)}) fusion(f32[512,1152]{1,0:T(8,128)S(1)} %copy-done.6, f32[1152]{0:T(1024)S(1)} %get-tuple-element.90, bf16[4608,1152]{1,0:T(8,128)(2,1)} %all-gather.14.cloned.1.call-done, f32[512,4608]{1,0:T(8,128)} %get-tuple-element.114), kind=kOutput, calls=%fused_computation.127 | convolution fusion | flops 5458821120 | bytes 25956864 | tf_op jit(solution)/shard_map/dot_general | solution.py:142
  322.4 39.6 %all-gather.16.cloned.1.call-done = bf16[1152,2048]{1,0:T(8,128)(2,1)} async-done(((bf16[72,2048]{1,0:T(8,128)(2,1)}), bf16[1152,2048]{1,0:T(8,128)(2,1)}) %all-gather.16.cloned.1.call-update) | async-done | bytes 4718608 | tf_op jit(solution)/shard_map/all_gather | solution.py:181
  362.1 8.6 fusion.54
  370.7 66.9 %all-gather.18.cloned.1.call-done = bf16[2048,2048]{1,0:T(8,128)(2,1)} async-done(((bf16[128,2048]{1,0:T(8,128)(2,1)}), bf16[2048,2048]{1,0:T(8,128)(2,1)}) %all-gather.18.cloned.1.call-update) | async-done | bytes 8388624 | tf_op jit(solution)/shard_map/all_gather | solution.py:182
  437.6 12.3 %fusion.55 = (bf16[2048,512]{0,1:T(8,128)(2,1)}, f32[512,2048]{1,0:T(8,128)}) fusion(bf16[2048,2048]{1,0:T(8,128)(2,1)} %all-gather.18.cloned.1.call-done, f32[512,2048]{1,0:T(8,128)} %get-tuple-element.116), kind=kOutput, calls=%fused_computation.77 | convolution fusion | flops 4305453056 | bytes 18874368 | tf_op jit(solution)/shard_map/dot_general | solution.py:142
  449.9 33.4 %all-gather.20.cloned.1.call-done = bf16[2048,768]{1,0:T(8,128)(2,1)} async-done(((bf16[128,768]{1,0:T(8,128)(2,1)}), bf16[2048,768]{1,0:T(8,128)(2,1)}) %all-gather.20.cloned.1.call-update) | async-done | bytes 3145744 | tf_op jit(solution)/shard_map/all_gather | solution.py:183
  496.8 8.9 fusion.39
  511.7 16.3 %fusion.12 = bf16[512,4608]{1,0:T(8,128)(2,1)} fusion(f32[512,4608]{1,0:T(8,128)} %get-tuple-element.114, bf16[512,1152]{1,0:T(8,128)(2,1)S(1)} %get-tuple-element.106, bf16[4608,1152]{1,0:T(8,128)(2,1)} %all-gather.14.cloned.1.call-done), kind=kOutput, calls=%fused_computation.20 | convolution fusion | flops 5483003904 | bytes 25952256 | tf_op jit(solution)/shard_map/ne,de->nd/dot_general | solution.py:146
  527.9 11.8 %multiply_reduce_fusion.2 = (f32[1152]{0:T(1024)S(1)}, f32[512]{0:T(512)S(1)}, f32[1152]{0:T(1024)S(1)}, f32[512,1152]{1,0:T(8,128)S(1)}) fusion(f32[512,1152]{1,0:T(8,128)S(1)} %copy-done.6, f32[512]{0:T(512)S(1)} %fusion.216, f32[512]{0:T(512)S(1)} %broadcast_multiply_fusion, f32[1152]{0:T(1024)S(1)} %get-tuple-element.92, ...), kind=kOutput, calls=%fused_computation.119 | convolution fusion | flops 5440534016 | bytes 20073984 | tf_op jit(solution)/shard_map/ne,de->nd/dot_general | solution.py:146
  550.0 15.6 %fusion.78 = f32[1024,16,72]{0,2,1:T(8,128)} fusion(bf16[512,16,72]{0,2,1:T(8,128)(2,1)S(1)} %bitcast.490, f32[16,512,1024]{2,1,0:T(8,128)} %get-tuple-element.101, f32[16,512]{1,0:T(8,128)S(1)} %copy-done.36), kind=kOutput, calls=%fused_computation.130 | convolution fusion | flops 1224736768 | bytes 39485440 | tf_op jit(solution)/shard_map/hqk,qhd->khd/dot_general | solution.py:262
  565.6 22.3 %multiply_reduce_fusion = (f32[16,512]{1,0:T(8,128)S(1)}, f32[16,512,1024]{2,1,0:T(8,128)}) fusion(f32[16,512,1024]{2,1,0:T(8,128)} %get-tuple-element.101, f32[16,512]{1,0:T(8,128)S(1)} %copy-done.36, bf16[512,16,72]{0,2,1:T(8,128)(2,1)S(1)} %bitcast.491, bf16[512,16,72]{0,2,1:T(8,128)(2,1)S(1)} %copy-done.24, bf16[512,16,72]{0,2,1:T(8,128)(2,1)S(1)} %copy-done.23), kind=kOutput, calls=%fused_computation.1 | convolution fusion | flops 1237835776 | bytes 70713344 | tf_op jit(solution)/shard_map/qhd,khd->hqk/dot_general | solution.py:253
  588.6 27.8 %multiply_convert_fusion = bf16[16,512,1024]{2,1,0:T(8,128)(2,1)} fusion(f32[16,512,1024]{2,1,0:T(8,128)} %get-tuple-element.110, f32[16,512,1024]{2,1,0:T(8,128)} %get-tuple-element.101, f32[16,512]{1,0:T(8,128)S(1)} %get-tuple-element.109, f32[16,512]{1,0:T(8,128)S(1)} %copy-done.36), kind=kLoop, calls=%fused_computation | loop fusion | flops 33554432 | bytes 83951616 | tf_op jit(solution)/shard_map/convert_element_type | solution.py:255
  616.5 11.4 %multiply_bitcast_fusion = f32[1024,16,72]{0,2,1:T(8,128)} fusion(bf16[16,512,1024]{2,1,0:T(8,128)(2,1)} %multiply_convert_fusion, bf16[512,3,16,72]{0,3,2,1:T(8,128)(2,1)} %bitcast.489), kind=kOutput, calls=%fused_computation.46 | convolution fusion | flops 1209139200 | bytes 22675456 | tf_op jit(solution)/shard_map/hqk,qhd->khd/dot_general | solution.py:260
  650.3 11.8 %constant_dynamic-slice_fusion.1 = (bf16[8,1,128,512]{2,1,0,3:T(2,128)(2,1)}, bf16[8,1,128,512]{2,1,0,3:T(2,128)(2,1)}, bf16[8,1,128,512]{2,1,0,3:T(2,128)(2,1)}, bf16[8,1,128,512]{2,1,0,3:T(2,128)(2,1)}) fusion(bf16[8,2,128,512]{2,1,0,3:T(2,128)(2,1)S(1)} %reshape.384, s32[]{:T(128)S(6)} %select_n.809, s32[]{:T(128)S(6)} %select_n.810, ...), kind=kLoop, calls=%fused_computation.374 | loop fusion | bytes 8388616 | tf_op jit(solution)/shard_map/jit(dynamic_index_in_dim)/dynamic_slice | solution.py:79
  691.0 10.4 fusion.100
  803.6 8.8 fusion.29
  834.5 9.1 collective-permute-done.64
  861.6 9.7 collective-permute-done.52
  886.6 9.3 collective-permute-done.56
  930.2 8.9 fusion.66
  1005.2 9.5 collective-permute-done.41
  1040.7 9.2 collective-permute-done.19
  1054.2 10.1 collective-permute-done.20
  1082.3 10.8 collective-permute-done.47
  (552 shorter events, 452.9 us)
Async XLA Ops:
  7.2 78.6 %all-gather.8.cloned.1.call-start = ((), (), s32[]{:S(2)}) async-start(), calls=%async_computation | async-start | bytes 8460288 | tf_op jit(solution)/shard_map/all_gather | solution.py:175
  8.0 153.1 %all-gather.10.cloned.1.call-start = ((), (), s32[]{:S(2)}) async-start(), calls=%async_computation.1 | async-start | bytes 2820096 | tf_op jit(solution)/shard_map/all_gather | solution.py:176
  8.7 210.6 %all-gather.12.cloned.1.call-start = ((), (), s32[]{:S(2)}) async-start(), calls=%async_computation.2 | async-start | bytes 11280384 | tf_op jit(solution)/shard_map/all_gather | solution.py:177
  9.4 298.9 %all-gather.14.cloned.1.call-start = ((), (), s32[]{:S(2)}) async-start(), calls=%async_computation.3 | async-start | bytes 11280384 | tf_op jit(solution)/shard_map/all_gather | solution.py:178
  10.0 352.1 %all-gather.16.cloned.1.call-start = ((), (), s32[]{:S(2)}) async-start(), calls=%async_computation.4 | async-start | bytes 5013504 | tf_op jit(solution)/shard_map/all_gather | solution.py:181
  10.6 427.0 %all-gather.18.cloned.1.call-start = ((), (), s32[]{:S(2)}) async-start(), calls=%async_computation.5 | async-start | bytes 8912896 | tf_op jit(solution)/shard_map/all_gather | solution.py:182
  11.2 472.2 %all-gather.20.cloned.1.call-start = ((), (), s32[]{:S(2)}) async-start(), calls=%async_computation.6 | async-start | bytes 3342336 | tf_op jit(solution)/shard_map/all_gather | solution.py:183
  168.0 543.8 %collective-permute-start.27 = (bf16[576,512]{1,0:T(8,128)(2,1)}, bf16[576,512]{1,0:T(8,128)(2,1)}, u32[]{:S(2)}, u32[]{:S(2)}) collective-permute-start(bf16[576,512]{1,0:T(8,128)(2,1)} %bitcast.49), channel_id=1, source_target_pairs={{0,1},{1,0},{2,3},{3,2},{4,5},{5,4},{6,7},{7,6},{8,9},{9,8},{10,11... | collective-permute-start | bytes 1769480 | tf_op jit(solution)/shard_map/ppermute | solution.py:18
  587.9 124.9 %collective-permute-start.28 = (bf16[512,1152]{1,0:T(8,128)(2,1)}, bf16[512,1152]{1,0:T(8,128)(2,1)}, u32[]{:S(2)}, u32[]{:S(2)}) collective-permute-start(bf16[512,1152]{1,0:T(8,128)(2,1)} %multiply_convert_fusion.6), channel_id=1, source_target_pairs={{0,1},{1,0},{2,3},{3,2},{4,5},{5,4},{6,7},{7,6},{8,9},{9,8},{10,11... | collective-permute-start | bytes 3538952 | tf_op jit(solution)/shard_map/ppermute | solution.py:18
  588.1 176.5 %collective-permute-start.61 = (bf16[512,2048]{1,0:T(8,128)(2,1)}, bf16[512,2048]{1,0:T(8,128)(2,1)}, u32[]{:S(2)}, u32[]{:S(2)}) collective-permute-start(bf16[512,2048]{1,0:T(8,128)(2,1)} %fusion.39), channel_id=1, source_target_pairs={{0,1},{1,0},{2,3},{3,2},{4,5},{5,4},{6,7},{7,6},{8,9},{9,8},{10,11... | collective-permute-start | bytes 6291464 | tf_op jit(solution)/shard_map/ppermute | solution.py:18
  588.4 113.0 %collective-permute-start.83 = (bf16[512,768]{1,0:T(8,128)(2,1)}, bf16[512,768]{1,0:T(8,128)(2,1)}, u32[]{:S(2)}, u32[]{:S(2)}) collective-permute-start(bf16[512,768]{1,0:T(8,128)(2,1)} %fusion.94), channel_id=1, source_target_pairs={{0,1},{1,0},{2,3},{3,2},{4,5},{5,4},{6,7},{7,6},{8,9},{9,8},{10,11... | collective-permute-start | bytes 2359304 | tf_op jit(solution)/shard_map/ppermute | solution.py:18
  667.9 33.5 %collective-permute-start.82 = (bf16[1024,512]{1,0:T(8,128)(2,1)}, bf16[1024,512]{1,0:T(8,128)(2,1)}, u32[]{:S(2)}, u32[]{:S(2)}) collective-permute-start(bf16[1024,512]{1,0:T(8,128)(2,1)} %bitcast.127), channel_id=1, source_target_pairs={{0,1},{1,0},{2,3},{3,2},{4,5},{5,4},{6,7},{7,6},{8,9},{9,8},{10,11... | collective-permute-start | bytes 3145736 | tf_op jit(solution)/shard_map/ppermute | solution.py:18
  710.2 63.3 %collective-permute-start.72 = (bf16[512,2048]{1,0:T(8,128)(2,1)S(1)}, bf16[512,2048]{1,0:T(8,128)(2,1)S(1)}, u32[]{:S(2)}, u32[]{:S(2)}) collective-permute-start(bf16[512,2048]{1,0:T(8,128)(2,1)S(1)} %copy-done.74), channel_id=1, source_target_pairs={{0,1},{1,0},{2,3},{3,2},{4,5},{5,4},{6,7},{7,6},{8,9},{9,8},{10,11... | collective-permute-start | bytes 6291464 | tf_op jit(solution)/shard_map/ppermute | solution.py:18
  711.8 52.2 %collective-permute-start.60 = (bf16[576,512]{1,0:T(8,128)(2,1)S(1)}, bf16[576,512]{1,0:T(8,128)(2,1)S(1)}, u32[]{:S(2)}, u32[]{:S(2)}) collective-permute-start(bf16[576,512]{1,0:T(8,128)(2,1)S(1)} %bitcast.573), channel_id=1, source_target_pairs={{0,1},{1,0},{2,3},{3,2},{4,5},{5,4},{6,7},{7,6},{8,9},{9,8},{10,11... | collective-permute-start | bytes 1769480 | tf_op jit(solution)/shard_map/ppermute | solution.py:18
  759.9 184.0 %collective-permute-start.39 = (bf16[512,4608]{1,0:T(8,128)(2,1)}, bf16[512,4608]{1,0:T(8,128)(2,1)}, u32[]{:S(2)}, u32[]{:S(2)}) collective-permute-start(bf16[512,4608]{1,0:T(8,128)(2,1)} %fusion.12), channel_id=1, source_target_pairs={{0,1},{1,0},{2,3},{3,2},{4,5},{5,4},{6,7},{7,6},{8,9},{9,8},{10,11... | collective-permute-start | bytes 14155784 | tf_op jit(solution)/shard_map/ppermute | solution.py:18
  763.9 37.0 %collective-permute-start.50 = (bf16[512,1152]{1,0:T(8,128)(2,1)S(1)}, bf16[512,1152]{1,0:T(8,128)(2,1)}, u32[]{:S(2)}, u32[]{:S(2)}) collective-permute-start(bf16[512,1152]{1,0:T(8,128)(2,1)S(1)} %copy-done.77), channel_id=1, source_target_pairs={{0,1},{1,0},{2,3},{3,2},{4,5},{5,4},{6,7},{7,6},{8,9},{9,8},{10,11... | collective-permute-start | bytes 3538952 | tf_op jit(solution)/shard_map/ppermute | solution.py:18
  764.0 160.5 %collective-permute-start.5 = (f32[2,512,16,72]{1,3,2,0:T(8,128)}, f32[2,512,16,72]{1,3,2,0:T(8,128)}, u32[]{:S(2)}, u32[]{:S(2)}) collective-permute-start(f32[2,512,16,72]{1,3,2,0:T(8,128)} %pad_maximum_fusion), channel_id=1, source_target_pairs={{0,1},{1,0},{2,3},{3,2},{4,5},{5,4},{6,7},{7,6},{8,9},{9,8},{10,11... | collective-permute-start | bytes 14155784 | tf_op jit(solution)/shard_map/ppermute | solution.py:18
  773.4 28.9 %collective-permute-start.49 = (bf16[2304,512]{1,0:T(8,128)(2,1)S(1)}, bf16[2304,512]{1,0:T(8,128)(2,1)S(1)}, u32[]{:S(2)}, u32[]{:S(2)}) collective-permute-start(bf16[2304,512]{1,0:T(8,128)(2,1)S(1)} %bitcast.565), channel_id=1, source_target_pairs={{0,1},{1,0},{2,3},{3,2},{4,5},{5,4},{6,7},{7,6},{8,9},{9,8},{10,11... | collective-permute-start | bytes 7077896 | tf_op jit(solution)/shard_map/ppermute | solution.py:18
  802.3 30.9 %collective-permute-start.67 = (bf16[72,2048]{1,0:T(8,128)(2,1)S(1)}, bf16[72,2048]{1,0:T(8,128)(2,1)}, u32[]{:S(2)}, u32[]{:S(2)}) collective-permute-start(bf16[72,2048]{1,0:T(8,128)(2,1)S(1)} %pad_maximum_fusion.20), channel_id=1, source_target_pairs={{0,2},{1,3},{4,0},{5,1},{8,4},{9,5},{12,8},{13,9},{14,12},{15,13},... | collective-permute-start | bytes 884744 | tf_op jit(solution)/shard_map/ppermute | solution.py:33
  852.4 24.8 %collective-permute-start.65 = (bf16[72,2048]{1,0:T(8,128)(2,1)S(1)}, bf16[72,2048]{1,0:T(8,128)(2,1)S(1)}, u32[]{:S(2)}, u32[]{:S(2)}) collective-permute-start(bf16[72,2048]{1,0:T(8,128)(2,1)S(1)} %get-tuple-element.46), channel_id=1, source_target_pairs={{0,4},{1,5},{4,8},{5,9},{8,12},{9,13},{12,14},{13,15},{14,10},{15,... | collective-permute-start | bytes 884744 | tf_op jit(solution)/shard_map/ppermute | solution.py:33
  885.2 21.3 %collective-permute-start.76 = (bf16[128,2048]{1,0:T(8,128)(2,1)S(1)}, bf16[128,2048]{1,0:T(8,128)(2,1)S(1)}, u32[]{:S(2)}, u32[]{:S(2)}) collective-permute-start(bf16[128,2048]{1,0:T(8,128)(2,1)S(1)} %get-tuple-element.38), channel_id=1, source_target_pairs={{0,4},{1,5},{4,8},{5,9},{8,12},{9,13},{12,14},{13,15},{14,10},{15,... | collective-permute-start | bytes 1572872 | tf_op jit(solution)/shard_map/ppermute | solution.py:33
  906.5 35.4 %collective-permute-start.38 = (bf16[576,512]{1,0:T(8,128)(2,1)S(1)}, bf16[576,512]{1,0:T(8,128)(2,1)}, u32[]{:S(2)}, u32[]{:S(2)}) collective-permute-start(bf16[576,512]{1,0:T(8,128)(2,1)S(1)} %bitcast.571), channel_id=1, source_target_pairs={{0,1},{1,0},{2,3},{3,2},{4,5},{5,4},{6,7},{7,6},{8,9},{9,8},{10,11... | collective-permute-start | bytes 1769480 | tf_op jit(solution)/shard_map/ppermute | solution.py:18
  910.6 89.0 %collective-permute-start.54 = (bf16[288,1152]{1,0:T(8,128)(2,1)}, bf16[288,1152]{1,0:T(8,128)(2,1)}, u32[]{:S(2)}, u32[]{:S(2)}) collective-permute-start(bf16[288,1152]{1,0:T(8,128)(2,1)} %get-tuple-element.30), channel_id=1, source_target_pairs={{0,4},{1,5},{4,8},{5,9},{8,12},{9,13},{12,14},{13,15},{14,10},{15,... | collective-permute-start | bytes 1990664 | tf_op jit(solution)/shard_map/ppermute | solution.py:33
  921.0 57.1 %collective-permute-start.81 = (bf16[128,2048]{1,0:T(8,128)(2,1)}, bf16[128,2048]{1,0:T(8,128)(2,1)}, u32[]{:S(2)}, u32[]{:S(2)}) collective-permute-start(bf16[128,2048]{1,0:T(8,128)(2,1)} %fusion.182), channel_id=1, source_target_pairs={{0,16},{16,0},{1,17},{17,1},{2,18},{18,2},{3,19},{19,3},{4,20},{20... | collective-permute-start | bytes 1572872 | tf_op jit(solution)/shard_map/ppermute | solution.py:22
  924.5 76.7 %collective-permute-start.58 = (bf16[288,1152]{1,0:T(8,128)(2,1)}, bf16[288,1152]{1,0:T(8,128)(2,1)}, u32[]{:S(2)}, u32[]{:S(2)}) collective-permute-start(bf16[288,1152]{1,0:T(8,128)(2,1)} %fusion.102), channel_id=1, source_target_pairs={{0,2},{1,3},{4,0},{5,1},{8,4},{9,5},{12,8},{13,9},{14,12},{15,13},... | collective-permute-start | bytes 1990664 | tf_op jit(solution)/shard_map/ppermute | solution.py:33
  969.2 52.5 %collective-permute-start.17 = (bf16[512,3456]{0,1:T(8,128)(2,1)}, bf16[512,3456]{0,1:T(8,128)(2,1)S(1)}, u32[]{:S(2)}, u32[]{:S(2)}) collective-permute-start(bf16[512,3456]{0,1:T(8,128)(2,1)} %bitcast.544), channel_id=1, source_target_pairs={{0,1},{1,0},{2,3},{3,2},{4,5},{5,4},{6,7},{7,6},{8,9},{9,8},{10,11... | collective-permute-start | bytes 10616840 | tf_op jit(solution)/shard_map/ppermute | solution.py:18
  977.4 44.2 %collective-permute-start.16 = (bf16[576,512]{1,0:T(8,128)(2,1)S(1)}, bf16[576,512]{1,0:T(8,128)(2,1)S(1)}, u32[]{:S(2)}, u32[]{:S(2)}) collective-permute-start(bf16[576,512]{1,0:T(8,128)(2,1)S(1)} %bitcast.576), channel_id=1, source_target_pairs={{0,1},{1,0},{2,3},{3,2},{4,5},{5,4},{6,7},{7,6},{8,9},{9,8},{10,11... | collective-permute-start | bytes 1769480 | tf_op jit(solution)/shard_map/ppermute | solution.py:18
  999.6 50.9 %collective-permute-start.45 = (bf16[72,4608]{1,0:T(8,128)(2,1)S(1)}, bf16[72,4608]{1,0:T(8,128)(2,1)}, u32[]{:S(2)}, u32[]{:S(2)}) collective-permute-start(bf16[72,4608]{1,0:T(8,128)(2,1)S(1)} %pad_maximum_fusion.12), channel_id=1, source_target_pairs={{0,2},{1,3},{4,0},{5,1},{8,4},{9,5},{12,8},{13,9},{14,12},{15,13},... | collective-permute-start | bytes 1990664 | tf_op jit(solution)/shard_map/ppermute | solution.py:33
  1014.9 35.7 %collective-permute-start.42 = (bf16[72,4608]{1,0:T(8,128)(2,1)S(1)}, bf16[72,4608]{1,0:T(8,128)(2,1)}, u32[]{:S(2)}, u32[]{:S(2)}) collective-permute-start(bf16[72,4608]{1,0:T(8,128)(2,1)S(1)} %fusion.109), channel_id=1, source_target_pairs={{0,4},{1,5},{4,8},{5,9},{8,12},{9,13},{12,14},{13,15},{14,10},{15,... | collective-permute-start | bytes 1990664 | tf_op jit(solution)/shard_map/ppermute | solution.py:33
  1053.7 28.6 %collective-permute-start.43 = (bf16[72,4608]{1,0:T(8,128)(2,1)S(1)}, bf16[72,4608]{1,0:T(8,128)(2,1)S(1)}, u32[]{:S(2)}, u32[]{:S(2)}) collective-permute-start(bf16[72,4608]{1,0:T(8,128)(2,1)S(1)} %get-tuple-element.36), channel_id=1, source_target_pairs={{0,4},{1,5},{4,8},{5,9},{8,12},{9,13},{12,14},{13,15},{14,10},{15,... | collective-permute-start | bytes 1990664 | tf_op jit(solution)/shard_map/ppermute | solution.py:33
  1069.6 23.5 %collective-permute-start.47 = (bf16[72,4608]{1,0:T(8,128)(2,1)S(1)}, bf16[72,4608]{1,0:T(8,128)(2,1)S(1)}, u32[]{:S(2)}, u32[]{:S(2)}) collective-permute-start(bf16[72,4608]{1,0:T(8,128)(2,1)S(1)} %fusion.108), channel_id=1, source_target_pairs={{0,2},{1,3},{4,0},{5,1},{8,4},{9,5},{12,8},{13,9},{14,12},{15,13},... | collective-permute-start | bytes 1990664 | tf_op jit(solution)/shard_map/ppermute | solution.py:33
  1071.6 23.6 %collective-permute-start.21 = (bf16[72,3456]{1,0:T(8,128)(2,1)S(1)}, bf16[72,3456]{1,0:T(8,128)(2,1)S(1)}, u32[]{:S(2)}, u32[]{:S(2)}) collective-permute-start(bf16[72,3456]{1,0:T(8,128)(2,1)S(1)} %get-tuple-element.44), channel_id=1, source_target_pairs={{0,4},{1,5},{4,8},{5,9},{8,12},{9,13},{12,14},{13,15},{14,10},{15,... | collective-permute-start | bytes 1493000 | tf_op jit(solution)/shard_map/ppermute | solution.py:33
  (157 other events, 2363.6 us)
Sparse Core Ops, SparseCore 0:
  10.2 75.5 all-gather.7
  87.9 41.6 all-gather.9
  131.9 87.3 all-gather.11
  221.5 86.8 all-gather.13
  310.5 51.5 all-gather.15
  364.1 73.4 all-gather.17
  439.9 43.4 all-gather.19
where the time goes:
time: 1130 us; the launch traced here: 1120 us
  waiting for transfers between devices  565 us (50%)
  matrix products  266 us (24%)
  local copies, waits for them, and re-layouts  92.7 us (8%)
  other arithmetic  92.5 us (8%)
  starting transfers between devices  88.8 us (8%)
  between operations  16.3 us (1%)
    ppermute x56, waiting for transfers between devices, hop(): return lax.ppermute(block, 'fsdp', pairs)  197 us
    all_gather x1, waiting for transfers between devices, shards(): lax.all_gather(w_fc2, 'fsdp', axis=0, tiled=True)  73.6 us
    dot_general x8, matrix products, product(): return jnp.dot(left, right, preferred_element_type=jnp.float32)  72 us
    all_gather x1, waiting for transfers between devices, shards(): lax.all_gather(w_proj2, 'fsdp', axis=0, tiled=True)  66.9 us
    dot_general x7, matrix products, input_grad(): jnp.einsum('ne,de->nd', grad, weight, preferred_element_type=jnp.float32)  59.2 us
    all_gather x1, waiting for transfers between devices, shards(): lax.all_gather(w_qkv, 'fsdp', axis=0, tiled=True)  58.8 us
    ppermute x56, starting transfers between devices, hop(): return lax.ppermute(block, 'fsdp', pairs)  57.3 us
    all_gather x1, waiting for transfers between devices, shards(): lax.all_gather(w_fc1, 'fsdp', axis=0, tiled=True)  51.1 us
  transfers between devices with their start and end apart: 100, of which 57 were waited for; matrix products, arithmetic and copies ran while one was open for 39% of the time, Pallas kernels for 0%

commit v1 on v0

--- a/solution.py
+++ b/solution.py
@@ -177,9 +177,37 @@
         lax.all_gather(w_fc1, "fsdp", axis=0, tiled=True),
         lax.all_gather(w_fc2, "fsdp", axis=0, tiled=True),
     )
+
+    def time_sources_all(x_in):
+        v_now, w_next, found_now = (lax.axis_size("fsdp"), lax.axis_index("fsdp"), x_in.shape[0])
+        side_arr = lax.dynamic_update_slice_in_dim(
+            jnp.zeros(
+                [pp * v_now if d == 0 else pp for d, pp in enumerate(x_in.shape)], x_in.dtype
+            ),
+            x_in,
+            w_next * found_now,
+            axis=0,
+        )
+        top = y = x_in
+        for dd in range(1, v_now // 2 + 1):
+            top = lax.ppermute(
+                top, axis_name="fsdp", perm=[(d, (d + 1) % v_now) for d in range(v_now)]
+            )
+            side_arr = lax.dynamic_update_slice_in_dim(
+                side_arr, top, (w_next - dd) % v_now * found_now, axis=0
+            )
+            if 2 * dd < v_now:
+                y = lax.ppermute(
+                    y, axis_name="fsdp", perm=[(d, (d - 1) % v_now) for d in range(v_now)]
+                )
+                side_arr = lax.dynamic_update_slice_in_dim(
+                    side_arr, y, (w_next + dd) % v_now * found_now, axis=0
+                )
+        return side_arr
+
     head_set = (
         lax.all_gather(w_proj1, "fsdp", axis=0, tiled=True),
-        lax.all_gather(w_proj2, "fsdp", axis=0, tiled=True),
+        time_sources_all(w_proj2),
         lax.all_gather(w_proj3, "fsdp", axis=0, tiled=True),
     )
     full_qkv, full_out, full_fc1, full_fc2 = block_set

time: 1130 us -> 1100 us (0.973)
  waiting for transfers between devices: 565 us -> 460 us
  starting transfers between devices: 88.8 us -> 130 us
  local copies, waits for them, and re-layouts: 92.7 us -> 122 us
    all_gather x1 -> x0, waiting for transfers between devices: 66.9 us -> none  [shards(): lax.all_gather(w_proj2, 'fsdp', axis=0, tiled=True)]
    all_gather x1, waiting for transfers between devices: 58.8 us -> 0.01 us  [shards(): lax.all_gather(w_qkv, 'fsdp', axis=0, tiled=True)]
    ppermute x0 -> x15, waiting for transfers between devices: none -> 44.4 us  [the longest x8 27.1 us: time_sources_all(): lax.ppermute(top, axis_name='fsdp', perm=[(d, (d + 1) % v_now) for d in r...]
    ppermute x0 -> x15, starting transfers between devices: none -> 37.6 us  [the longest x7 20.1 us: time_sources_all(): lax.ppermute(y, axis_name='fsdp', perm=[(d, (d - 1) % v_now) for d in ran...]
    dynamic_update_slice x0 -> x16, local copies, waits for them, and re-layouts: none -> 20.8 us  [the longest x8 11 us: time_sources_all(): lax.dynamic_update_slice_in_dim(side_arr, top, (w_next - dd) % v_now * fo...]
    all_gather x1, waiting for transfers between devices: 51.1 us -> 34.9 us  [shards(): lax.all_gather(w_fc1, 'fsdp', axis=0, tiled=True)]
    unnamed x182 -> x180, local copies, waits for them, and re-layouts: 31.1 us -> 36.4 us
  transfers between devices with their start and end apart: 100 -> 114, of which waited for: 57 -> 62; matrix products, arithmetic and copies ran while one was open for 39% -> 43% of each run, Pallas kernels for 0% -> 0%
where the time goes in v1:
time: 1100 us; the launch traced here: 1090 us
  waiting for transfers between devices  460 us (42%)
  matrix products  263 us (24%)
  starting transfers between devices  130 us (12%)
  local copies, waits for them, and re-layouts  122 us (11%)
  other arithmetic  94.1 us (9%)
  between operations  16.1 us (1%)
    ppermute x56, waiting for transfers between devices, hop(): return lax.ppermute(block, 'fsdp', pairs)  194 us
    all_gather x1, waiting for transfers between devices, shards(): lax.all_gather(w_fc2, 'fsdp', axis=0, tiled=True)  74.8 us
    dot_general x8, matrix products, product(): return jnp.dot(left, right, preferred_element_type=jnp.float32)  67.8 us
    dot_general x7, matrix products, input_grad(): jnp.einsum('ne,de->nd', grad, weight, preferred_element_type=jnp.float32)  61.3 us
    ppermute x56, starting transfers between devices, hop(): return lax.ppermute(block, 'fsdp', pairs)  56.5 us
    dot_general x7, matrix products, chip_grad(): total = jnp.dot(rows, grads, preferred_element_type=jnp.float32)  42.7 us
    all_gather x1, waiting for transfers between devices, shards(): lax.all_gather(w_proj1, 'fsdp', axis=0, tiled=True)  39.9 us
    unnamed x180, local copies, waits for them, and re-layouts  36.4 us
  transfers between devices with their start and end apart: 114, of which 62 were waited for; matrix products, arithmetic and copies ran while one was open for 43% of the time, Pallas kernels for 0%

profile of v1, /device:TPU:0, one launch (start us, length us, event | category | flops | bytes accessed | tf_op | source)
XLA Modules:
  0.0 1086.4 jit_solution(1570695205966443167)
XLA Ops:
  36.8 9.4 collective-permute-done.7
  96.5 9.7 collective-permute-done.13
  106.2 10.0 convolution_convert_fusion
  167.7 16.9 %fusion.244 = (f32[16,512]{1,0:T(8,128)S(1)}, f32[16,512,1024]{2,1,0:T(8,128)}) fusion(bf16[512,16,72]{0,2,1:T(8,128)(2,1)S(1)} %get-tuple-element.67, bf16[512,16,72]{0,2,1:T(8,128)(2,1)S(1)} %get-tuple-element.54, bf16[512,3,16,72]{0,3,2,1:T(8,128)(2,1)} %bitcast.488, pred[512,1024]{1,0:T(8,128)(4,1)S(1)} %broadcast_compare_fusion), kind=kOutput, calls=%fused_computation.468 | convolution fusion | flops 1237835776 | bytes 37650432 | tf_op jit(solution)/shard_map/qhd,khd->hqk/dot_general | solution.py:227
  184.6 14.4 %fusion = f32[16,512]{1,0:T(8,128)S(1)} fusion(f32[16,512,1024]{2,1,0:T(8,128)} %get-tuple-element.101, f32[16,512]{1,0:T(8,128)S(1)} %get-tuple-element.100), kind=kLoop, calls=%fused_computation.6 | loop fusion | flops 16769024 | bytes 33619968 | tf_op jit(solution)/shard_map/reduce_sum | solution.py:231
  199.6 15.8 %fusion.98 = bf16[16,72,512]{2,1,0:T(8,128)(2,1)S(1)} fusion(f32[16,512,1024]{2,1,0:T(8,128)} %get-tuple-element.101, f32[16,512]{1,0:T(8,128)S(1)} %fusion, f32[16,512]{1,0:T(8,128)S(1)} %get-tuple-element.100, bf16[512,16,72]{0,2,1:T(8,128)(2,1)} %get-tuple-element.66, bf16[512,16,72]{0,2,1:T(8,128)(2,1)} %get-tuple-element.52), kind=kOutput, calls=%fused_computation.150 | convolution fusion | flops 1238433792 | bytes 37158912 | tf_op jit(solution)/shard_map/hqk,khd->qhd/dot_general | solution.py:234
  222.5 34.9 %all-gather.11.cloned.1.call-done = bf16[1152,4608]{1,0:T(8,128)(2,1)} async-done(((bf16[72,4608]{1,0:T(8,128)(2,1)}), bf16[1152,4608]{1,0:T(8,128)(2,1)}) %all-gather.11.cloned.1.call-update) | async-done | bytes 10616848 | tf_op jit(solution)/shard_map/all_gather | solution.py:177
  257.4 14.2 %fusion.20 = (bf16[4608,512]{0,1:T(8,128)(2,1)}, f32[512,4608]{1,0:T(8,128)}) fusion(bf16[1152,4608]{1,0:T(8,128)(2,1)} %all-gather.11.cloned.1.call-done, f32[512,1152]{1,0:T(8,128)} %copy-done.5, f32[1152]{0:T(1024)S(1)} %get-tuple-element.91, f32[1152]{0:T(1024)S(1)} %get-tuple-element.92, f32[512]{0:T(512)S(1)} %fusion.216, ...), kind=kOutput, calls=%fused_computation.28 | convolution fusion | flops 5460000768 | bytes 27145216 | tf_op jit(solution)/shard_map/dot_general | solution.py:142
  271.6 74.8 %all-gather.13.cloned.1.call-done = bf16[4608,1152]{1,0:T(8,128)(2,1)} async-done(((bf16[288,1152]{1,0:T(8,128)(2,1)}), bf16[4608,1152]{1,0:T(8,128)(2,1)}) %all-gather.13.cloned.1.call-update) | async-done | bytes 10616848 | tf_op jit(solution)/shard_map/all_gather | solution.py:178
  346.4 13.9 %add_convert_fusion = (bf16[512,1152]{1,0:T(8,128)(2,1)S(1)}, f32[512,1152]{1,0:T(8,128)}) fusion(f32[512,1152]{1,0:T(8,128)} %copy-done.5, f32[1152]{0:T(1024)S(1)} %get-tuple-element.90, bf16[4608,1152]{1,0:T(8,128)(2,1)} %all-gather.13.cloned.1.call-done, f32[512,4608]{1,0:T(8,128)} %get-tuple-element.114), kind=kOutput, calls=%fused_computation.127 | convolution fusion | flops 5458821120 | bytes 25956864 | tf_op jit(solution)/shard_map/dot_general | solution.py:142
  360.3 39.9 %all-gather.15.cloned.1.call-done = bf16[1152,2048]{1,0:T(8,128)(2,1)} async-done(((bf16[72,2048]{1,0:T(8,128)(2,1)}), bf16[1152,2048]{1,0:T(8,128)(2,1)}) %all-gather.15.cloned.1.call-update) | async-done | bytes 4718608 | tf_op jit(solution)/shard_map/all_gather | solution.py:209
  409.2 10.5 fusion.55
  419.7 26.3 %all-gather.17.cloned.1.call-done = bf16[2048,768]{1,0:T(8,128)(2,1)} async-done(((bf16[128,768]{1,0:T(8,128)(2,1)}), bf16[2048,768]{1,0:T(8,128)(2,1)}) %all-gather.17.cloned.1.call-update) | async-done | bytes 3145744 | tf_op jit(solution)/shard_map/all_gather | solution.py:211
  458.0 11.3 %fusion.39 = bf16[512,2048]{1,0:T(8,128)(2,1)} fusion(f32[512,2048]{1,0:T(8,128)} %copy-done.81, bf16[512,2048]{1,0:T(8,128)(2,1)S(1)} %fusion.36, bf16[2048,2048]{1,0:T(8,128)(2,1)} %constant_dynamic-update-slice_fusion), kind=kOutput, calls=%fused_computation.53 | convolution fusion | flops 4305453056 | bytes 16777216 | tf_op jit(solution)/shard_map/ne,de->nd/dot_general | solution.py:146
  473.8 17.0 %fusion.12 = bf16[512,4608]{1,0:T(8,128)(2,1)} fusion(f32[512,4608]{1,0:T(8,128)} %get-tuple-element.114, bf16[512,1152]{1,0:T(8,128)(2,1)S(1)} %get-tuple-element.106, bf16[4608,1152]{1,0:T(8,128)(2,1)} %all-gather.13.cloned.1.call-done), kind=kOutput, calls=%fused_computation.20 | convolution fusion | flops 5483003904 | bytes 25952256 | tf_op jit(solution)/shard_map/ne,de->nd/dot_general | solution.py:146
  490.8 11.6 %multiply_reduce_fusion.2 = (f32[1152]{0:T(1024)S(1)}, f32[512]{0:T(512)S(1)}, f32[1152]{0:T(1024)S(1)}, f32[512,1152]{1,0:T(8,128)S(1)}) fusion(f32[512,1152]{1,0:T(8,128)S(1)} %copy-done.6, f32[512]{0:T(512)S(1)} %fusion.216, f32[512]{0:T(512)S(1)} %broadcast_multiply_fusion, f32[1152]{0:T(1024)S(1)} %get-tuple-element.92, ...), kind=kOutput, calls=%fused_computation.119 | convolution fusion | flops 5440534016 | bytes 20073984 | tf_op jit(solution)/shard_map/ne,de->nd/dot_general | solution.py:146
  514.1 15.7 %fusion.78 = f32[1024,16,72]{0,2,1:T(8,128)} fusion(bf16[512,16,72]{0,2,1:T(8,128)(2,1)S(1)} %bitcast.490, f32[16,512,1024]{2,1,0:T(8,128)} %get-tuple-element.101, f32[16,512]{1,0:T(8,128)S(1)} %copy-done.33), kind=kOutput, calls=%fused_computation.130 | convolution fusion | flops 1224736768 | bytes 39485440 | tf_op jit(solution)/shard_map/hqk,qhd->khd/dot_general | solution.py:290
  529.9 22.3 %multiply_reduce_fusion = (f32[16,512]{1,0:T(8,128)S(1)}, f32[16,512,1024]{2,1,0:T(8,128)}) fusion(f32[16,512,1024]{2,1,0:T(8,128)} %get-tuple-element.101, f32[16,512]{1,0:T(8,128)S(1)} %copy-done.33, bf16[512,16,72]{0,2,1:T(8,128)(2,1)S(1)} %bitcast.491, bf16[512,16,72]{0,2,1:T(8,128)(2,1)S(1)} %copy-done.20, bf16[512,16,72]{0,2,1:T(8,128)(2,1)S(1)} %copy-done.19), kind=kOutput, calls=%fused_computation.1 | convolution fusion | flops 1237835776 | bytes 70713344 | tf_op jit(solution)/shard_map/qhd,khd->hqk/dot_general | solution.py:281
  552.9 27.8 %multiply_convert_fusion = bf16[16,512,1024]{2,1,0:T(8,128)(2,1)} fusion(f32[16,512,1024]{2,1,0:T(8,128)} %get-tuple-element.110, f32[16,512,1024]{2,1,0:T(8,128)} %get-tuple-element.101, f32[16,512]{1,0:T(8,128)S(1)} %get-tuple-element.109, f32[16,512]{1,0:T(8,128)S(1)} %copy-done.33), kind=kLoop, calls=%fused_computation | loop fusion | flops 33554432 | bytes 83951616 | tf_op jit(solution)/shard_map/convert_element_type | solution.py:283
  580.7 11.3 %multiply_bitcast_fusion = f32[1024,16,72]{0,2,1:T(8,128)} fusion(bf16[16,512,1024]{2,1,0:T(8,128)(2,1)} %multiply_convert_fusion, bf16[512,3,16,72]{0,3,2,1:T(8,128)(2,1)} %bitcast.489), kind=kOutput, calls=%fused_computation.46 | convolution fusion | flops 1209139200 | bytes 22675456 | tf_op jit(solution)/shard_map/hqk,qhd->khd/dot_general | solution.py:288
  615.5 12.0 %constant_dynamic-slice_fusion.1 = (bf16[8,1,128,512]{2,1,0,3:T(2,128)(2,1)}, bf16[8,1,128,512]{2,1,0,3:T(2,128)(2,1)}, bf16[8,1,128,512]{2,1,0,3:T(2,128)(2,1)}, bf16[8,1,128,512]{2,1,0,3:T(2,128)(2,1)}) fusion(bf16[8,2,128,512]{2,1,0,3:T(2,128)(2,1)} %reshape.384, s32[]{:T(128)S(6)} %select_n.948, s32[]{:T(128)S(6)} %select_n.949, ...), kind=kLoop, calls=%fused_computation.374 | loop fusion | bytes 8388616 | tf_op jit(solution)/shard_map/jit(dynamic_index_in_dim)/dynamic_slice | solution.py:79
  658.9 9.0 fusion.100
  768.9 8.6 fusion.29
  799.4 9.1 collective-permute-done.79
  826.9 10.0 collective-permute-done.67
  853.1 8.9 collective-permute-done.71
  895.3 8.9 fusion.66
  908.7 8.5 fusion.21
  970.8 8.7 collective-permute-done.56
  1006.2 9.2 collective-permute-done.34
  1020.0 9.8 collective-permute-done.35
  1047.8 11.1 %collective-permute-done.62 = bf16[72,4608]{1,0:T(8,128)(2,1)S(1)} collective-permute-done((bf16[72,4608]{1,0:T(8,128)(2,1)S(1)}, bf16[72,4608]{1,0:T(8,128)(2,1)S(1)}, u32[]{:S(2)}, u32[]{:S(2)}) %collective-permute-start.62) | collective-permute-done | bytes 663584 | tf_op jit(solution)/shard_map/ppermute | solution.py:33
  (593 shorter events, 548.7 us)
Async XLA Ops:
  7.2 98.9 %all-gather.7.cloned.1.call-start = ((), (), s32[]{:S(2)}) async-start(), calls=%async_computation | async-start | bytes 8460288 | tf_op jit(solution)/shard_map/all_gather | solution.py:175
  7.9 207.5 %all-gather.9.cloned.1.call-start = ((), (), s32[]{:S(2)}) async-start(), calls=%async_computation.1 | async-start | bytes 2820096 | tf_op jit(solution)/shard_map/all_gather | solution.py:176
  8.7 248.7 %all-gather.11.cloned.1.call-start = ((), (), s32[]{:S(2)}) async-start(), calls=%async_computation.2 | async-start | bytes 11280384 | tf_op jit(solution)/shard_map/all_gather | solution.py:177
  9.4 337.0 %all-gather.13.cloned.1.call-start = ((), (), s32[]{:S(2)}) async-start(), calls=%async_computation.3 | async-start | bytes 11280384 | tf_op jit(solution)/shard_map/all_gather | solution.py:178
  10.0 390.1 %all-gather.15.cloned.1.call-start = ((), (), s32[]{:S(2)}) async-start(), calls=%async_computation.4 | async-start | bytes 5013504 | tf_op jit(solution)/shard_map/all_gather | solution.py:209
  10.6 435.5 %all-gather.17.cloned.1.call-start = ((), (), s32[]{:S(2)}) async-start(), calls=%async_computation.5 | async-start | bytes 3342336 | tf_op jit(solution)/shard_map/all_gather | solution.py:211
  18.6 45.7 %collective-permute-start.29 = (f32[1,1152]{1,0:T(1,128)S(1)}, f32[1,1152]{1,0:T(1,128)S(1)}, u32[]{:S(2)}, u32[]{:S(2)}) collective-permute-start(f32[1,1152]{1,0:T(1,128)S(1)} %get-tuple-element.22), channel_id=1, source_target_pairs={{0,16},{16,0},{1,17},{17,1},{2,18},{18,2},{3,19},{19,3},{4,20},{20... | collective-permute-start | bytes 13832 | tf_op jit(solution)/shard_map/ppermute | solution.py:22
  36.8 30.9 %collective-permute-start.8 = (bf16[128,2048]{1,0:T(8,128)(2,1)}, bf16[128,2048]{1,0:T(8,128)(2,1)S(1)}, u32[]{:S(2)}, u32[]{:S(2)}) collective-permute-start(bf16[128,2048]{1,0:T(8,128)(2,1)} %collective-permute-done.6), channel_id=1, source_target_pairs={{0,15},{1,0},{2,1},{3,2},{4,3},{5,4},{6,5},{7,6},{8,7},{9,8},{10,9... | collective-permute-start | bytes 1572872 | tf_op jit(solution)/shard_map/ppermute | solution.py:200
  95.2 32.9 %collective-permute-start.14 = (bf16[128,2048]{1,0:T(8,128)(2,1)}, bf16[128,2048]{1,0:T(8,128)(2,1)}, u32[]{:S(2)}, u32[]{:S(2)}) collective-permute-start(bf16[128,2048]{1,0:T(8,128)(2,1)} %collective-permute-done.12), channel_id=1, source_target_pairs={{0,15},{1,0},{2,1},{3,2},{4,3},{5,4},{6,5},{7,6},{8,7},{9,8},{10,9... | collective-permute-start | bytes 1572872 | tf_op jit(solution)/shard_map/ppermute | solution.py:200
  106.1 28.3 %collective-permute-start.15 = (bf16[128,2048]{1,0:T(8,128)(2,1)}, bf16[128,2048]{1,0:T(8,128)(2,1)S(1)}, u32[]{:S(2)}, u32[]{:S(2)}) collective-permute-start(bf16[128,2048]{1,0:T(8,128)(2,1)} %collective-permute-done.13), channel_id=1, source_target_pairs={{0,1},{1,2},{2,3},{3,4},{4,5},{5,6},{6,7},{7,8},{8,9},{9,10},{10,1... | collective-permute-start | bytes 1572872 | tf_op jit(solution)/shard_map/ppermute | solution.py:193
  125.2 41.2 %collective-permute-start.4 = (bf16[2,512,16,72]{1,3,2,0:T(8,128)(2,1)S(1)}, bf16[2,512,16,72]{1,3,2,0:T(8,128)(2,1)S(1)}, u32[]{:S(2)}, u32[]{:S(2)}) collective-permute-start(bf16[2,512,16,72]{1,3,2,0:T(8,128)(2,1)S(1)} %pad_maximum_fusion.2), channel_id=1, source_target_pairs={{0,1},{1,0},{2,3},{3,2},{4,5},{5,4},{6,7},{7,6},{8,9},{9,8},{10,11... | collective-permute-start | bytes 7077896 | tf_op jit(solution)/shard_map/ppermute | solution.py:18
  222.4 456.0 %collective-permute-start.42 = (bf16[576,512]{1,0:T(8,128)(2,1)}, bf16[576,512]{1,0:T(8,128)(2,1)}, u32[]{:S(2)}, u32[]{:S(2)}) collective-permute-start(bf16[576,512]{1,0:T(8,128)(2,1)} %bitcast.49), channel_id=1, source_target_pairs={{0,1},{1,0},{2,3},{3,2},{4,5},{5,4},{6,7},{7,6},{8,9},{9,8},{10,11... | collective-permute-start | bytes 1769480 | tf_op jit(solution)/shard_map/ppermute | solution.py:18
  552.2 127.1 %collective-permute-start.43 = (bf16[512,1152]{1,0:T(8,128)(2,1)}, bf16[512,1152]{1,0:T(8,128)(2,1)}, u32[]{:S(2)}, u32[]{:S(2)}) collective-permute-start(bf16[512,1152]{1,0:T(8,128)(2,1)} %multiply_convert_fusion.6), channel_id=1, source_target_pairs={{0,1},{1,0},{2,3},{3,2},{4,5},{5,4},{6,7},{7,6},{8,9},{9,8},{10,11... | collective-permute-start | bytes 3538952 | tf_op jit(solution)/shard_map/ppermute | solution.py:18
  552.4 178.3 %collective-permute-start.76 = (bf16[512,2048]{1,0:T(8,128)(2,1)}, bf16[512,2048]{1,0:T(8,128)(2,1)}, u32[]{:S(2)}, u32[]{:S(2)}) collective-permute-start(bf16[512,2048]{1,0:T(8,128)(2,1)} %fusion.39), channel_id=1, source_target_pairs={{0,1},{1,0},{2,3},{3,2},{4,5},{5,4},{6,7},{7,6},{8,9},{9,8},{10,11... | collective-permute-start | bytes 6291464 | tf_op jit(solution)/shard_map/ppermute | solution.py:18
  552.7 115.3 %collective-permute-start.98 = (bf16[512,768]{1,0:T(8,128)(2,1)}, bf16[512,768]{1,0:T(8,128)(2,1)}, u32[]{:S(2)}, u32[]{:S(2)}) collective-permute-start(bf16[512,768]{1,0:T(8,128)(2,1)} %fusion.94), channel_id=1, source_target_pairs={{0,1},{1,0},{2,3},{3,2},{4,5},{5,4},{6,7},{7,6},{8,9},{9,8},{10,11... | collective-permute-start | bytes 2359304 | tf_op jit(solution)/shard_map/ppermute | solution.py:18
  633.7 34.2 %collective-permute-start.97 = (bf16[1024,512]{1,0:T(8,128)(2,1)}, bf16[1024,512]{1,0:T(8,128)(2,1)}, u32[]{:S(2)}, u32[]{:S(2)}) collective-permute-start(bf16[1024,512]{1,0:T(8,128)(2,1)} %bitcast.127), channel_id=1, source_target_pairs={{0,1},{1,0},{2,3},{3,2},{4,5},{5,4},{6,7},{7,6},{8,9},{9,8},{10,11... | collective-permute-start | bytes 3145736 | tf_op jit(solution)/shard_map/ppermute | solution.py:18
  676.7 62.0 %collective-permute-start.87 = (bf16[512,2048]{1,0:T(8,128)(2,1)S(1)}, bf16[512,2048]{1,0:T(8,128)(2,1)S(1)}, u32[]{:S(2)}, u32[]{:S(2)}) collective-permute-start(bf16[512,2048]{1,0:T(8,128)(2,1)S(1)} %copy-done.73), channel_id=1, source_target_pairs={{0,1},{1,0},{2,3},{3,2},{4,5},{5,4},{6,7},{7,6},{8,9},{9,8},{10,11... | collective-permute-start | bytes 6291464 | tf_op jit(solution)/shard_map/ppermute | solution.py:18
  678.3 51.9 %collective-permute-start.75 = (bf16[576,512]{1,0:T(8,128)(2,1)S(1)}, bf16[576,512]{1,0:T(8,128)(2,1)S(1)}, u32[]{:S(2)}, u32[]{:S(2)}) collective-permute-start(bf16[576,512]{1,0:T(8,128)(2,1)S(1)} %bitcast.573), channel_id=1, source_target_pairs={{0,1},{1,0},{2,3},{3,2},{4,5},{5,4},{6,7},{7,6},{8,9},{9,8},{10,11... | collective-permute-start | bytes 1769480 | tf_op jit(solution)/shard_map/ppermute | solution.py:18
  726.1 182.7 %collective-permute-start.54 = (bf16[512,4608]{1,0:T(8,128)(2,1)}, bf16[512,4608]{1,0:T(8,128)(2,1)}, u32[]{:S(2)}, u32[]{:S(2)}) collective-permute-start(bf16[512,4608]{1,0:T(8,128)(2,1)} %fusion.12), channel_id=1, source_target_pairs={{0,1},{1,0},{2,3},{3,2},{4,5},{5,4},{6,7},{7,6},{8,9},{9,8},{10,11... | collective-permute-start | bytes 14155784 | tf_op jit(solution)/shard_map/ppermute | solution.py:18
  730.1 36.9 %collective-permute-start.65 = (bf16[512,1152]{1,0:T(8,128)(2,1)S(1)}, bf16[512,1152]{1,0:T(8,128)(2,1)}, u32[]{:S(2)}, u32[]{:S(2)}) collective-permute-start(bf16[512,1152]{1,0:T(8,128)(2,1)S(1)} %copy-done.77), channel_id=1, source_target_pairs={{0,1},{1,0},{2,3},{3,2},{4,5},{5,4},{6,7},{7,6},{8,9},{9,8},{10,11... | collective-permute-start | bytes 3538952 | tf_op jit(solution)/shard_map/ppermute | solution.py:18
  730.2 160.3 %collective-permute-start.20 = (f32[2,512,16,72]{1,3,2,0:T(8,128)}, f32[2,512,16,72]{1,3,2,0:T(8,128)}, u32[]{:S(2)}, u32[]{:S(2)}) collective-permute-start(f32[2,512,16,72]{1,3,2,0:T(8,128)} %pad_maximum_fusion), channel_id=1, source_target_pairs={{0,1},{1,0},{2,3},{3,2},{4,5},{5,4},{6,7},{7,6},{8,9},{9,8},{10,11... | collective-permute-start | bytes 14155784 | tf_op jit(solution)/shard_map/ppermute | solution.py:18
  738.6 29.7 %collective-permute-start.64 = (bf16[2304,512]{1,0:T(8,128)(2,1)S(1)}, bf16[2304,512]{1,0:T(8,128)(2,1)}, u32[]{:S(2)}, u32[]{:S(2)}) collective-permute-start(bf16[2304,512]{1,0:T(8,128)(2,1)S(1)} %bitcast.565), channel_id=1, source_target_pairs={{0,1},{1,0},{2,3},{3,2},{4,5},{5,4},{6,7},{7,6},{8,9},{9,8},{10,11... | collective-permute-start | bytes 7077896 | tf_op jit(solution)/shard_map/ppermute | solution.py:18
  768.2 30.6 %collective-permute-start.82 = (bf16[72,2048]{1,0:T(8,128)(2,1)}, bf16[72,2048]{1,0:T(8,128)(2,1)}, u32[]{:S(2)}, u32[]{:S(2)}) collective-permute-start(bf16[72,2048]{1,0:T(8,128)(2,1)} %pad_maximum_fusion.20), channel_id=1, source_target_pairs={{0,2},{1,3},{4,0},{5,1},{8,4},{9,5},{12,8},{13,9},{14,12},{15,13},... | collective-permute-start | bytes 884744 | tf_op jit(solution)/shard_map/ppermute | solution.py:33
  871.0 36.0 %collective-permute-start.53 = (bf16[576,512]{1,0:T(8,128)(2,1)S(1)}, bf16[576,512]{1,0:T(8,128)(2,1)}, u32[]{:S(2)}, u32[]{:S(2)}) collective-permute-start(bf16[576,512]{1,0:T(8,128)(2,1)S(1)} %bitcast.571), channel_id=1, source_target_pairs={{0,1},{1,0},{2,3},{3,2},{4,5},{5,4},{6,7},{7,6},{8,9},{9,8},{10,11... | collective-permute-start | bytes 1769480 | tf_op jit(solution)/shard_map/ppermute | solution.py:18
  876.5 89.1 %collective-permute-start.69 = (bf16[288,1152]{1,0:T(8,128)(2,1)}, bf16[288,1152]{1,0:T(8,128)(2,1)}, u32[]{:S(2)}, u32[]{:S(2)}) collective-permute-start(bf16[288,1152]{1,0:T(8,128)(2,1)} %get-tuple-element.30), channel_id=1, source_target_pairs={{0,4},{1,5},{4,8},{5,9},{8,12},{9,13},{12,14},{13,15},{14,10},{15,... | collective-permute-start | bytes 1990664 | tf_op jit(solution)/shard_map/ppermute | solution.py:33
  886.8 56.0 %collective-permute-start.96 = (bf16[128,2048]{1,0:T(8,128)(2,1)}, bf16[128,2048]{1,0:T(8,128)(2,1)}, u32[]{:S(2)}, u32[]{:S(2)}) collective-permute-start(bf16[128,2048]{1,0:T(8,128)(2,1)} %fusion.182), channel_id=1, source_target_pairs={{0,16},{16,0},{1,17},{17,1},{2,18},{18,2},{3,19},{19,3},{4,20},{20... | collective-permute-start | bytes 1572872 | tf_op jit(solution)/shard_map/ppermute | solution.py:22
  890.5 76.3 %collective-permute-start.73 = (bf16[288,1152]{1,0:T(8,128)(2,1)}, bf16[288,1152]{1,0:T(8,128)(2,1)}, u32[]{:S(2)}, u32[]{:S(2)}) collective-permute-start(bf16[288,1152]{1,0:T(8,128)(2,1)} %fusion.102), channel_id=1, source_target_pairs={{0,2},{1,3},{4,0},{5,1},{8,4},{9,5},{12,8},{13,9},{14,12},{15,13},... | collective-permute-start | bytes 1990664 | tf_op jit(solution)/shard_map/ppermute | solution.py:33
  934.0 53.2 %collective-permute-start.32 = (bf16[512,3456]{0,1:T(8,128)(2,1)}, bf16[512,3456]{0,1:T(8,128)(2,1)S(1)}, u32[]{:S(2)}, u32[]{:S(2)}) collective-permute-start(bf16[512,3456]{0,1:T(8,128)(2,1)} %bitcast.544), channel_id=1, source_target_pairs={{0,1},{1,0},{2,3},{3,2},{4,5},{5,4},{6,7},{7,6},{8,9},{9,8},{10,11... | collective-permute-start | bytes 10616840 | tf_op jit(solution)/shard_map/ppermute | solution.py:18
  942.2 45.0 %collective-permute-start.31 = (bf16[576,512]{1,0:T(8,128)(2,1)S(1)}, bf16[576,512]{1,0:T(8,128)(2,1)S(1)}, u32[]{:S(2)}, u32[]{:S(2)}) collective-permute-start(bf16[576,512]{1,0:T(8,128)(2,1)S(1)} %bitcast.576), channel_id=1, source_target_pairs={{0,1},{1,0},{2,3},{3,2},{4,5},{5,4},{6,7},{7,6},{8,9},{9,8},{10,11... | collective-permute-start | bytes 1769480 | tf_op jit(solution)/shard_map/ppermute | solution.py:18
  965.6 50.8 %collective-permute-start.60 = (bf16[72,4608]{1,0:T(8,128)(2,1)}, bf16[72,4608]{1,0:T(8,128)(2,1)}, u32[]{:S(2)}, u32[]{:S(2)}) collective-permute-start(bf16[72,4608]{1,0:T(8,128)(2,1)} %pad_maximum_fusion.12), channel_id=1, source_target_pairs={{0,2},{1,3},{4,0},{5,1},{8,4},{9,5},{12,8},{13,9},{14,12},{15,13},... | collective-permute-start | bytes 1990664 | tf_op jit(solution)/shard_map/ppermute | solution.py:33
  980.5 35.9 %collective-permute-start.57 = (bf16[72,4608]{1,0:T(8,128)(2,1)}, bf16[72,4608]{1,0:T(8,128)(2,1)}, u32[]{:S(2)}, u32[]{:S(2)}) collective-permute-start(bf16[72,4608]{1,0:T(8,128)(2,1)} %fusion.109), channel_id=1, source_target_pairs={{0,4},{1,5},{4,8},{5,9},{8,12},{9,13},{12,14},{13,15},{14,10},{15,... | collective-permute-start | bytes 1990664 | tf_op jit(solution)/shard_map/ppermute | solution.py:33
  1019.2 28.6 %collective-permute-start.58 = (bf16[72,4608]{1,0:T(8,128)(2,1)S(1)}, bf16[72,4608]{1,0:T(8,128)(2,1)S(1)}, u32[]{:S(2)}, u32[]{:S(2)}) collective-permute-start(bf16[72,4608]{1,0:T(8,128)(2,1)S(1)} %get-tuple-element.36), channel_id=1, source_target_pairs={{0,4},{1,5},{4,8},{5,9},{8,12},{9,13},{12,14},{13,15},{14,10},{15,... | collective-permute-start | bytes 1990664 | tf_op jit(solution)/shard_map/ppermute | solution.py:33
  (170 other events, 2610.0 us)
Sparse Core Ops, SparseCore 0:
  10.2 94.8 all-gather.6
  107.3 55.5 all-gather.8
  165.1 92.2 all-gather.10
  259.5 86.8 all-gather.12
  348.6 51.5 all-gather.14
  402.3 43.7 all-gather.16
